TPU v7x, 32 devices: a whole 2x2x4 slice. The times are simulated.
32 devices in a mesh: ctx: 16 (over z, x, core), fsdp: 2 (over y).
Axes of the slice: x: 2, y: 2, z: 4, core: 2. Of those that a mesh axis runs over, the one named last changes fastest.
Arguments:
- tokens: bfloat16 [2, 4096, 768], P('fsdp', 'ctx'), may hold values from -6 to 6
- query_weight: bfloat16 [768, 768], P('fsdp'), may hold values from -0.21875 to 0.21875
- query_bias: bfloat16 [768], P('fsdp'), may hold values from -1.5 to 1.5
- key_weight: bfloat16 [768, 768], P('fsdp'), may hold values from -0.21875 to 0.21875
- value_weight: bfloat16 [768, 768], P('fsdp'), may hold values from -0.21875 to 0.21875
- value_bias: bfloat16 [768], P('fsdp'), may hold values from -1.5 to 1.5
- out_weight: bfloat16 [768, 768], P('fsdp'), may hold values from -1.25 to 1.25
- out_bias: bfloat16 [768], P('fsdp'), may hold values from -1.5 to 1.5
- first_gain: bfloat16 [768], P('fsdp'), may hold values from 0.5 to 1.5
- first_shift: bfloat16 [768], P('fsdp'), may hold values from -1.5 to 1.5
- inner_weight: bfloat16 [768, 3072], P('fsdp'), may hold values from -0.21875 to 0.21875
- inner_bias: bfloat16 [3072], P('fsdp'), may hold values from -1.5 to 1.5
- outer_weight: bfloat16 [3072, 768], P('fsdp'), may hold values from -0.109375 to 0.109375
- outer_bias: bfloat16 [768], P('fsdp'), may hold values from -1.5 to 1.5
- second_gain: bfloat16 [768], P('fsdp'), may hold values from 0.5 to 1.5
- second_shift: bfloat16 [768], P('fsdp'), may hold values from -1.5 to 1.5
- doc_lengths: int32 [2, 48], P('fsdp'), may hold values from 1 to 2304, 4096 in all within a row
- grad_output: bfloat16 [2, 4096, 768], P('fsdp', 'ctx'), may hold values from -6 to 6
Outputs:
- output: bfloat16 [2, 4096, 768], P('fsdp', 'ctx')
- grad_tokens: float32 [2, 4096, 768], P('fsdp', 'ctx')
- grad_query_weight: float32 [768, 768], P('fsdp')
- grad_query_bias: float32 [768], P('fsdp')
- grad_key_weight: float32 [768, 768], P('fsdp')
- grad_value_weight: float32 [768, 768], P('fsdp')
- grad_value_bias: float32 [768], P('fsdp')
- grad_out_weight: float32 [768, 768], P('fsdp')
- grad_out_bias: float32 [768], P('fsdp')
- grad_first_gain: float32 [768], P('fsdp')
- grad_first_shift: float32 [768], P('fsdp')
- grad_inner_weight: float32 [768, 3072], P('fsdp')
- grad_inner_bias: float32 [3072], P('fsdp')
- grad_outer_weight: float32 [3072, 768], P('fsdp')
- grad_outer_bias: float32 [768], P('fsdp')
- grad_second_gain: float32 [768], P('fsdp')
- grad_second_shift: float32 [768], P('fsdp')
Inputs may be any that keep to these rules, and one draw needn't show every extreme that they name: `doc_lengths`: each row holds the 48 document lengths of one sequence in order; they sum to 4096 and the longest is exactly 2304.
All inputs are finite; a program needn't handle non-finite values.
Results may differ from a plain program's by a relative error of at most 0.018.
Values may be sent and summed in bfloat16 or wider, within the bound.
No kernel may reach another device: no remote copies, remote signals or barrier semaphores. Data moves between devices by JAX's collectives and lax.ppermute only.
A program may use at most 384 MiB of HBM per device.

v0:
```python
import math
import jax
import jax.numpy as jnp
from jax import lax
from jax.sharding import PartitionSpec as P

H = 12
HD = 64
eps = 1e-12


def layer_norm(r, gain, shift):
    mean = jnp.mean(r, axis=-1, keepdims=True)
    centered = r - mean
    var = jnp.mean(centered * centered, axis=-1, keepdims=True)
    return centered * lax.rsqrt(var + eps) * gain + shift


def gelu_exact(v):
    return jax.nn.gelu(v, approximate=False)


def inner_rows(left, right):
    return lax.dot_general(
        left, right, (((1,), (1,)), ((), ())), preferred_element_type=jnp.float32
    )


def inner_cols(left, right):
    return lax.dot_general(
        left, right, (((0,), (0,)), ((), ())), preferred_element_type=jnp.float32
    )


def segment_of(places, lengths):
    ends = jnp.cumsum(lengths)
    return jnp.sum((places[:, None] >= ends[None, :]).astype(jnp.int32), axis=1)


def masked_scores(query_part, key_part, allowed, scale):
    raw = inner_rows(query_part, key_part) * scale
    return jnp.where(allowed, raw, jnp.float32(-1e30))


def on_device(
    tokens,
    query_weight,
    query_bias,
    key_weight,
    value_weight,
    value_bias,
    out_weight,
    out_bias,
    first_gain,
    first_shift,
    inner_weight,
    inner_bias,
    outer_weight,
    outer_bias,
    second_gain,
    second_shift,
    doc_lengths,
    grad_output,
):
    rows = tokens.shape[1]
    width = tokens.shape[2]
    scale = 1.0 / math.sqrt(HD)
    length_total = rows * lax.axis_size("ctx")
    gathered = (
        lax.all_gather(query_weight, "fsdp", axis=0, tiled=True),
        lax.all_gather(query_bias, "fsdp", axis=0, tiled=True),
        lax.all_gather(key_weight, "fsdp", axis=0, tiled=True),
        lax.all_gather(value_weight, "fsdp", axis=0, tiled=True),
        lax.all_gather(value_bias, "fsdp", axis=0, tiled=True),
        lax.all_gather(out_weight, "fsdp", axis=0, tiled=True),
        lax.all_gather(out_bias, "fsdp", axis=0, tiled=True),
        lax.all_gather(first_gain, "fsdp", axis=0, tiled=True),
        lax.all_gather(first_shift, "fsdp", axis=0, tiled=True),
        lax.all_gather(inner_weight, "fsdp", axis=0, tiled=True),
        lax.all_gather(inner_bias, "fsdp", axis=0, tiled=True),
        lax.all_gather(outer_weight, "fsdp", axis=0, tiled=True),
        lax.all_gather(outer_bias, "fsdp", axis=0, tiled=True),
        lax.all_gather(second_gain, "fsdp", axis=0, tiled=True),
        lax.all_gather(second_shift, "fsdp", axis=0, tiled=True),
    )
    (
        query_full,
        qbias_full,
        key_full,
        value_full,
        vbias_full,
        out_full,
        obias_full,
        gain_one,
        shift_one,
        inner_full,
        ibias_full,
        outer_full,
        outbias_full,
        gain_two,
        shift_two,
    ) = gathered
    local_in = tokens[0]
    local_float = local_in.astype(jnp.float32)
    query_low = (
        jnp.dot(local_in, query_full, preferred_element_type=jnp.float32)
        + qbias_full.astype(jnp.float32)
    ).astype(jnp.bfloat16)
    key_low = jnp.dot(local_in, key_full, preferred_element_type=jnp.float32).astype(jnp.bfloat16)
    value_low = (
        jnp.dot(local_in, value_full, preferred_element_type=jnp.float32)
        + vbias_full.astype(jnp.float32)
    ).astype(jnp.bfloat16)
    first_row = lax.axis_index("ctx") * rows
    places_own = first_row + jnp.arange(rows, dtype=jnp.int32)
    segs_own = segment_of(places_own, doc_lengths[0])
    keys_all, values_all = (
        lax.all_gather(key_low, "ctx", axis=0, tiled=True),
        lax.all_gather(value_low, "ctx", axis=0, tiled=True),
    )
    places_all = jnp.arange(length_total, dtype=jnp.int32)
    segs_all = segment_of(places_all, doc_lengths[0])
    allowed = segs_own[:, None] == segs_all[None, :]
    head_outs = []
    log_list = []
    for head in range(H):
        cols = slice(head * HD, (head + 1) * HD)
        scores = masked_scores(query_low[:, cols], keys_all[:, cols], allowed, scale)
        top = jnp.max(scores, axis=1, keepdims=True)
        expd = jnp.exp(scores - top)
        total = jnp.sum(expd, axis=1, keepdims=True)
        probs_low = (expd / total).astype(jnp.bfloat16)
        head_outs.append(
            jnp.dot(probs_low, values_all[:, cols], preferred_element_type=jnp.float32)
        )
        log_list.append(top[:, 0] + jnp.log(total[:, 0]))
    attn_low = jnp.concatenate(head_outs, axis=1).astype(jnp.bfloat16)
    log_sums = jnp.stack(log_list, axis=0)
    branch = jnp.dot(attn_low, out_full, preferred_element_type=jnp.float32) + obias_full.astype(
        jnp.float32
    )
    hidden, first_back = jax.vjp(
        layer_norm,
        local_float + branch,
        gain_one.astype(jnp.float32),
        shift_one.astype(jnp.float32),
    )
    hidden_low = hidden.astype(jnp.bfloat16)
    inner = jnp.dot(hidden_low, inner_full, preferred_element_type=jnp.float32) + ibias_full.astype(
        jnp.float32
    )
    active, gelu_back = jax.vjp(gelu_exact, inner)
    active_low = active.astype(jnp.bfloat16)
    outer = jnp.dot(
        active_low, outer_full, preferred_element_type=jnp.float32
    ) + outbias_full.astype(jnp.float32)
    result, second_back = jax.vjp(
        layer_norm, hidden + outer, gain_two.astype(jnp.float32), shift_two.astype(jnp.float32)
    )
    output = result.astype(jnp.bfloat16)[None]
    grad_y = grad_output[0].astype(jnp.float32)
    d_second, grad_gain_two, grad_shift_two = second_back(grad_y)
    d_outer_low = d_second.astype(jnp.bfloat16)
    grad_outbias = jnp.sum(d_outer_low.astype(jnp.float32), axis=0)
    grad_outer = inner_cols(active_low, d_outer_low)
    d_active = inner_rows(d_outer_low, outer_full)
    (d_inner,) = gelu_back(d_active)
    d_inner_low = d_inner.astype(jnp.bfloat16)
    grad_ibias = jnp.sum(d_inner_low.astype(jnp.float32), axis=0)
    grad_inner = inner_cols(hidden_low, d_inner_low)
    d_hidden = d_second + inner_rows(d_inner_low, inner_full)
    d_first, grad_gain_one, grad_shift_one = first_back(d_hidden)
    d_branch_low = d_first.astype(jnp.bfloat16)
    grad_obias = jnp.sum(d_branch_low.astype(jnp.float32), axis=0)
    grad_out = inner_cols(attn_low, d_branch_low)
    d_attn_low = inner_rows(d_branch_low, out_full).astype(jnp.bfloat16)
    dq_list = []
    dk_list = []
    dv_list = []
    for head in range(H):
        cols = slice(head * HD, (head + 1) * HD)
        scores = masked_scores(query_low[:, cols], keys_all[:, cols], allowed, scale)
        probs = jnp.exp(scores - log_sums[head][:, None])
        d_probs = inner_rows(d_attn_low[:, cols], values_all[:, cols])
        delta = jnp.sum(probs * d_probs, axis=1)
        d_scores = (probs * (d_probs - delta[:, None])).astype(jnp.bfloat16)
        dq_list.append(
            jnp.dot(d_scores, keys_all[:, cols], preferred_element_type=jnp.float32) * scale
        )
        dk_list.append(inner_cols(d_scores, query_low[:, cols]) * scale)
        dv_list.append(inner_cols(probs.astype(jnp.bfloat16), d_attn_low[:, cols]))
    key_terms = jnp.concatenate(dk_list + dv_list, axis=1)
    shares = lax.psum_scatter(
        key_terms.astype(jnp.bfloat16), "ctx", scatter_dimension=0, tiled=True
    ).astype(jnp.float32)
    d_key_low = shares[:, :width].astype(jnp.bfloat16)
    d_value_low = shares[:, width:].astype(jnp.bfloat16)
    d_query_low = jnp.concatenate(dq_list, axis=1).astype(jnp.bfloat16)
    grad_qbias = jnp.sum(d_query_low.astype(jnp.float32), axis=0)
    grad_vbias = jnp.sum(d_value_low.astype(jnp.float32), axis=0)
    grad_query = inner_cols(local_in, d_query_low)
    grad_key = inner_cols(local_in, d_key_low)
    grad_value = inner_cols(local_in, d_value_low)
    grad_input = (
        d_first
        + inner_rows(d_query_low, query_full)
        + inner_rows(d_key_low, key_full)
        + inner_rows(d_value_low, value_full)
    )
    shards = (
        lax.psum_scatter(
            grad_query.astype(jnp.bfloat16), "fsdp", scatter_dimension=0, tiled=True
        ).astype(jnp.float32),
        lax.psum_scatter(
            grad_qbias.astype(jnp.bfloat16), "fsdp", scatter_dimension=0, tiled=True
        ).astype(jnp.float32),
        lax.psum_scatter(
            grad_key.astype(jnp.bfloat16), "fsdp", scatter_dimension=0, tiled=True
        ).astype(jnp.float32),
        lax.psum_scatter(
            grad_value.astype(jnp.bfloat16), "fsdp", scatter_dimension=0, tiled=True
        ).astype(jnp.float32),
        lax.psum_scatter(
            grad_vbias.astype(jnp.bfloat16), "fsdp", scatter_dimension=0, tiled=True
        ).astype(jnp.float32),
        lax.psum_scatter(
            grad_out.astype(jnp.bfloat16), "fsdp", scatter_dimension=0, tiled=True
        ).astype(jnp.float32),
        lax.psum_scatter(
            grad_obias.astype(jnp.bfloat16), "fsdp", scatter_dimension=0, tiled=True
        ).astype(jnp.float32),
        lax.psum_scatter(
            grad_gain_one.astype(jnp.bfloat16), "fsdp", scatter_dimension=0, tiled=True
        ).astype(jnp.float32),
        lax.psum_scatter(
            grad_shift_one.astype(jnp.bfloat16), "fsdp", scatter_dimension=0, tiled=True
        ).astype(jnp.float32),
        lax.psum_scatter(
            grad_inner.astype(jnp.bfloat16), "fsdp", scatter_dimension=0, tiled=True
        ).astype(jnp.float32),
        lax.psum_scatter(
            grad_ibias.astype(jnp.bfloat16), "fsdp", scatter_dimension=0, tiled=True
        ).astype(jnp.float32),
        lax.psum_scatter(
            grad_outer.astype(jnp.bfloat16), "fsdp", scatter_dimension=0, tiled=True
        ).astype(jnp.float32),
        lax.psum_scatter(
            grad_outbias.astype(jnp.bfloat16), "fsdp", scatter_dimension=0, tiled=True
        ).astype(jnp.float32),
        lax.psum_scatter(
            grad_gain_two.astype(jnp.bfloat16), "fsdp", scatter_dimension=0, tiled=True
        ).astype(jnp.float32),
        lax.psum_scatter(
            grad_shift_two.astype(jnp.bfloat16), "fsdp", scatter_dimension=0, tiled=True
        ).astype(jnp.float32),
    )
    totals = lax.psum(tuple(shards), "ctx")
    return (output, grad_input[None]) + tuple(totals)


def solution(mesh):
    placed = (
        P("fsdp", "ctx", None),
        P("fsdp", None),
        P("fsdp"),
        P("fsdp", None),
        P("fsdp", None),
        P("fsdp"),
        P("fsdp", None),
        P("fsdp"),
        P("fsdp"),
        P("fsdp"),
        P("fsdp", None),
        P("fsdp"),
        P("fsdp", None),
        P("fsdp"),
        P("fsdp"),
        P("fsdp"),
        P("fsdp", None),
        P("fsdp", "ctx", None),
    )
    return jax.shard_map(
        on_device,
        mesh=mesh,
        in_specs=placed,
        out_specs=(
            P("fsdp", "ctx", None),
            P("fsdp", "ctx", None),
            P("fsdp", None),
            P("fsdp"),
            P("fsdp", None),
            P("fsdp", None),
            P("fsdp"),
            P("fsdp", None),
            P("fsdp"),
            P("fsdp"),
            P("fsdp"),
            P("fsdp", None),
            P("fsdp"),
            P("fsdp", None),
            P("fsdp"),
            P("fsdp"),
            P("fsdp"),
        ),
        check_vma=False,
    )
```

profile of v0, /device:TPU:1, one launch (start us, length us, event | category | flops | bytes accessed | tf_op | source)
XLA Modules:
  0.0 1196.2 jit_solution(10272641338332044763)
XLA Ops:
  9.5 25.0 %all-gather.20.cloned.1.call-done = bf16[768,768]{1,0:T(8,128)(2,1)} async-done(((bf16[384,768]{1,0:T(8,128)(2,1)}), bf16[768,768]{1,0:T(8,128)(2,1)}) %all-gather.20.cloned.1.call-update) | async-done | bytes 1179664 | tf_op jit(solution)/shard_map/all_gather | solution.py:72
  38.0 3.2 all-gather.1
  41.2 17.6 %all-gather.24.cloned.1.call-done = bf16[768,768]{1,0:T(8,128)(2,1)} async-done(((bf16[384,768]{1,0:T(8,128)(2,1)}), bf16[768,768]{1,0:T(8,128)(2,1)}) %all-gather.24.cloned.1.call-update) | async-done | bytes 1179664 | tf_op jit(solution)/shard_map/all_gather | solution.py:73
  63.6 3.2 all-gather.6
  66.9 3.2 all-gather.5
  70.1 3.5 all-gather.2
  73.7 3.5 all-gather
  77.8 3.5 all-gather.4
  81.4 3.2 all-gather.3
  84.6 3.2 all-gather.7
  87.9 3.7 all-gather.8
  93.4 54.9 %all-gather.22.cloned.1.call-done = bf16[4096,768]{1,0:T(8,128)(2,1)} async-done(((bf16[256,768]{1,0:T(8,128)(2,1)}), bf16[4096,768]{1,0:T(8,128)(2,1)}) %all-gather.22.cloned.1.call-update) | async-done | bytes 6291472 | tf_op jit(solution)/shard_map/all_gather | solution.py:118
  151.2 3.1 fusion.293
  155.0 2.9 fusion.294
  158.6 3.3 fusion.295
  162.6 2.9 fusion.296
  166.2 3.1 fusion.297
  170.1 2.9 fusion.298
  173.7 3.3 fusion.299
  177.7 3.0 fusion.300
  181.4 3.1 fusion.301
  185.3 2.9 fusion.302
  188.9 3.1 fusion.303
  194.7 16.8 %all-gather.26.cloned.1.call-done = bf16[4096,768]{1,0:T(8,128)(2,1)} async-done(((bf16[256,768]{1,0:T(8,128)(2,1)}), bf16[4096,768]{1,0:T(8,128)(2,1)}) %all-gather.26.cloned.1.call-update) | async-done | bytes 6291472 | tf_op jit(solution)/shard_map/all_gather | solution.py:119
  211.5 3.6 fusion.146
  243.4 54.8 %all-gather.30.cloned.1.call-done = bf16[768,3072]{1,0:T(8,128)(2,1)} async-done(((bf16[384,3072]{1,0:T(8,128)(2,1)}), bf16[768,3072]{1,0:T(8,128)(2,1)}) %all-gather.30.cloned.1.call-update) | async-done | bytes 4718608 | tf_op jit(solution)/shard_map/all_gather | solution.py:79
  298.2 11.5 multiply_convert_fusion.12
  309.7 52.7 %all-gather.32.cloned.1.call-done = bf16[3072,768]{1,0:T(8,128)(2,1)} async-done(((bf16[1536,768]{1,0:T(8,128)(2,1)}), bf16[3072,768]{1,0:T(8,128)(2,1)}) %all-gather.32.cloned.1.call-update) | async-done | bytes 4718608 | tf_op jit(solution)/shard_map/all_gather | solution.py:81
  362.4 4.0 fusion.305
  368.5 2.7 fusion.287
  389.6 3.2 multiply_reduce_fusion.8
  392.8 4.9 multiply_convert_fusion.8
  397.7 3.0 multiply_reduce_fusion.7
  400.7 4.9 multiply_convert_fusion.7
  405.5 4.4 multiply_reduce_fusion.6
  410.0 4.9 multiply_convert_fusion.6
  414.8 4.2 multiply_reduce_fusion.5
  419.0 4.8 multiply_convert_fusion.5
  423.8 5.6 multiply_reduce_fusion.4
  429.4 6.4 multiply_convert_fusion.4
  435.8 5.3 multiply_reduce_fusion.3
  441.1 6.0 multiply_convert_fusion.3
  447.1 5.6 multiply_reduce_fusion.2
  452.6 5.9 multiply_convert_fusion.2
  458.6 5.3 multiply_reduce_fusion.1
  463.9 6.0 multiply_convert_fusion.1
  469.9 5.6 multiply_reduce_fusion
  475.5 5.9 multiply_convert_fusion
  481.4 3.1 fusion.3
  484.6 3.1 fusion.5
  523.8 4.1 fusion.113
  530.3 2.9 fusion.117
  535.6 2.9 fusion.121
  549.4 5.2 convolution_convert_fusion.1
  556.6 3.6 convolution_convert_fusion
  560.3 93.9 %reduce-scatter.14.cloned.1.call-done = bf16[256,1536]{0,1:T(8,128)(2,1)} async-done(((bf16[4096,1536]{0,1:T(8,128)(2,1)}), bf16[256,1536]{0,1:T(8,128)(2,1)}) %reduce-scatter.14.cloned.1.call-update) | async-done | bytes 786448 | tf_op jit(solution)/shard_map/reduce_scatter | solution.py:193
  668.9 9.7 reduce-scatter.22.cloned.1.call-done
  679.9 22.8 %reduce-scatter.16.cloned.1.call-done = bf16[384,768]{1,0:T(8,128)(2,1)} async-done(((bf16[768,768]{1,0:T(8,128)(2,1)}), bf16[384,768]{1,0:T(8,128)(2,1)}) %reduce-scatter.16.cloned.1.call-update) | async-done | bytes 589840 | tf_op jit(solution)/shard_map/reduce_scatter | solution.py:226
  702.7 62.7 %reduce-scatter.18.cloned.1.call-done = bf16[384,3072]{1,0:T(8,128)(2,1)} async-done(((bf16[768,3072]{1,0:T(8,128)(2,1)}), bf16[384,3072]{1,0:T(8,128)(2,1)}) %reduce-scatter.18.cloned.1.call-update) | async-done | bytes 2359312 | tf_op jit(solution)/shard_map/reduce_scatter | solution.py:238
  765.4 63.0 %reduce-scatter.20.cloned.1.call-done = bf16[1536,768]{1,0:T(8,128)(2,1)} async-done(((bf16[3072,768]{1,0:T(8,128)(2,1)}), bf16[1536,768]{1,0:T(8,128)(2,1)}) %reduce-scatter.20.cloned.1.call-update) | async-done | bytes 2359312 | tf_op jit(solution)/shard_map/reduce_scatter | solution.py:244
  828.6 6.1 all-reduce.10
  841.4 11.6 reduce-scatter.24.cloned.1.call-done
  854.4 23.1 %reduce-scatter.26.cloned.1.call-done = bf16[384,768]{1,0:T(8,128)(2,1)} async-done(((bf16[768,768]{1,0:T(8,128)(2,1)}), bf16[384,768]{1,0:T(8,128)(2,1)}) %reduce-scatter.26.cloned.1.call-update) | async-done | bytes 589840
  878.8 303.9 %all-reduce.12 = (f32[384,768]{0,1:T(8,128)}, f32[384]{0:T(512)}, f32[384,768]{0,1:T(8,128)}, f32[384,768]{0,1:T(8,128)S(1)}, f32[384]{0:T(512)}, /*index=5*/f32...) all-reduce(bf16[384,768]{0,1:T(8,128)(2,1)S(1)} %copy.52, ...), channel_id=1, replica_groups=mesh['ctx'=16,'fsdp'=2] {'ctx'}, use_global_device_ids=true, to_apply=%region_49.50 | all-reduce | flops 3543552 | bytes 21270528 | tf_op jit(solution)/shard_map/psum | solution.py:257
  (387 shorter events, 158.8 us)
Async XLA Ops:
  7.2 27.3 %all-gather.20.cloned.1.call-start = ((), (), s32[]{:S(2)}) async-start(), calls=%async_computation.8 | async-start | bytes 1769472 | tf_op jit(solution)/shard_map/all_gather | solution.py:72
  7.9 50.9 %all-gather.24.cloned.1.call-start = ((), (), s32[]{:S(2)}) async-start(), calls=%async_computation.10 | async-start | bytes 1769472 | tf_op jit(solution)/shard_map/all_gather | solution.py:73
  8.7 82.9 %all-gather.18.cloned.1.call-start = ((), (), s32[]{:S(2)}) async-start(), calls=%async_computation.7 | async-start | bytes 1769472 | tf_op jit(solution)/shard_map/all_gather | solution.py:70
  9.4 138.9 %all-gather.22.cloned.1.call-start = ((), (), s32[]{:S(2)}) async-start(), calls=%async_computation.9 | async-start | bytes 6684672 | tf_op jit(solution)/shard_map/all_gather | solution.py:118
  37.1 26.5 %copy-start.82 = (bf16[384]{0:T(512)(128)(2,1)S(1)}, bf16[384]{0:T(512)(128)(2,1)}, u32[]{:S(2)}) copy-start(bf16[384]{0:T(512)(128)(2,1)} %param.31) | copy-start | bytes 2308
  37.1 29.7 %copy-start.81 = (bf16[1536]{0:T(1024)(128)(2,1)S(1)}, bf16[1536]{0:T(1024)(128)(2,1)}, u32[]{:S(2)}) copy-start(bf16[1536]{0:T(1024)(128)(2,1)} %param.29) | copy-start | bytes 9220
  37.1 33.0 %copy-start.83 = (bf16[384]{0:T(512)(128)(2,1)S(1)}, bf16[384]{0:T(512)(128)(2,1)}, u32[]{:S(2)}) copy-start(bf16[384]{0:T(512)(128)(2,1)} %param.25) | copy-start | bytes 2308
  37.1 36.6 %copy-start.84 = (bf16[384]{0:T(512)(128)(2,1)S(1)}, bf16[384]{0:T(512)(128)(2,1)}, u32[]{:S(2)}) copy-start(bf16[384]{0:T(512)(128)(2,1)} %param.20) | copy-start | bytes 2308
  37.1 40.1 %copy-start.89 = (s32[1,48]{1,0:T(1,128)S(1)}, s32[1,48]{1,0:T(1,128)}, u32[]{:S(2)}) copy-start(s32[1,48]{1,0:T(1,128)} %param.34) | copy-start | bytes 580
  37.1 40.7 %copy-start.85 = (bf16[384]{0:T(512)(128)(2,1)S(1)}, bf16[384]{0:T(512)(128)(2,1)}, u32[]{:S(2)}) copy-start(bf16[384]{0:T(512)(128)(2,1)} %param.27) | copy-start | bytes 2308
  37.1 44.2 %copy-start.86 = (bf16[384]{0:T(512)(128)(2,1)S(1)}, bf16[384]{0:T(512)(128)(2,1)}, u32[]{:S(2)}) copy-start(bf16[384]{0:T(512)(128)(2,1)} %param.26) | copy-start | bytes 2308
  37.2 47.4 %copy-start.87 = (bf16[384]{0:T(512)(128)(2,1)S(1)}, bf16[384]{0:T(512)(128)(2,1)}, u32[]{:S(2)}) copy-start(bf16[384]{0:T(512)(128)(2,1)} %param.32) | copy-start | bytes 2308
  37.2 50.7 %copy-start.88 = (bf16[384]{0:T(512)(128)(2,1)S(1)}, bf16[384]{0:T(512)(128)(2,1)}, u32[]{:S(2)}) copy-start(bf16[384]{0:T(512)(128)(2,1)} %param.33) | copy-start | bytes 2308
  37.2 54.4 %copy-start.57 = (bf16[1,256,768]{2,1,0:T(8,128)(2,1)S(1)}, bf16[1,256,768]{2,1,0:T(8,128)(2,1)}, u32[]{:S(2)}) copy-start(bf16[1,256,768]{2,1,0:T(8,128)(2,1)} %param.18) | copy-start | bytes 1179652
  37.2 174.3 %all-gather.26.cloned.1.call-start = ((), (), s32[]{:S(2)}) async-start(), calls=%async_computation.11 | async-start | bytes 6684672 | tf_op jit(solution)/shard_map/all_gather | solution.py:119
  61.5 179.4 %all-gather.28.cloned.1.call-start = ((), (), s32[]{:S(2)}) async-start(), calls=%async_computation.12 | async-start | bytes 1769472 | tf_op jit(solution)/shard_map/all_gather | solution.py:75
  62.0 236.2 %all-gather.30.cloned.1.call-start = ((), (), s32[]{:S(2)}) async-start(), calls=%async_computation.13 | async-start | bytes 7077888 | tf_op jit(solution)/shard_map/all_gather | solution.py:79
  62.8 299.6 %all-gather.32.cloned.1.call-start = ((), (), s32[]{:S(2)}) async-start(), calls=%async_computation.14 | async-start | bytes 7077888 | tf_op jit(solution)/shard_map/all_gather | solution.py:81
  63.5 590.6 %reduce-scatter.14.cloned.1.call-start = ((), (), s32[]{:S(2)}) async-start(), calls=%async_computation.15 | async-start | bytes 13369344 | tf_op jit(solution)/shard_map/reduce_scatter | solution.py:193
  93.4 57.8 %copy-start.78 = (bf16[256,768]{1,0:T(8,128)(2,1)}, bf16[256,768]{1,0:T(8,128)(2,1)S(1)}, u32[]{:S(2)}) copy-start(bf16[256,768]{1,0:T(8,128)(2,1)S(1)} %fusion.108) | copy-start | bytes 1179652
  211.5 5.6 copy-start.35
  240.9 57.3 %copy-start.75 = (bf16[256,768]{0,1:T(8,128)(2,1)}, bf16[256,768]{0,1:T(8,128)(2,1)S(1)}, u32[]{:S(2)}) copy-start(bf16[256,768]{0,1:T(8,128)(2,1)S(1)} %fusion.157) | copy-start | bytes 1179652
  309.7 56.7 %copy-start.69 = (bf16[256,3072]{1,0:T(8,128)(2,1)}, bf16[256,3072]{1,0:T(8,128)(2,1)S(1)}, u32[]{:S(2)}) copy-start(bf16[256,3072]{1,0:T(8,128)(2,1)S(1)} %get-tuple-element.124) | copy-start | bytes 4718596
  362.4 6.0 slice-start.6
  362.4 4.3 copy-start.68
  362.4 6.0 slice-start.7
  362.4 6.0 copy-start.91
  367.1 9.4 slice-start.2
  368.2 4.2 slice-start.4
  368.5 8.0 slice-start.3
  377.3 28.2 %copy-start.59 = (bf16[256,768]{1,0:T(8,128)(2,1)}, bf16[256,768]{1,0:T(8,128)(2,1)S(1)}, u32[]{:S(2)}) copy-start(bf16[256,768]{1,0:T(8,128)(2,1)S(1)} %convolution_convert_fusion.18) | copy-start | bytes 1179652
  392.8 4.9 copy-start.13
  400.7 4.9 copy-start.16
  410.0 4.9 copy-start.19
  481.4 6.2 copy-start.39
  481.4 6.2 copy-start.79
  481.4 7.7 copy-start.41
  484.6 5.8 copy-start.43
  487.7 4.2 copy-start.45
  490.4 4.3 copy-start.49
  491.8 4.2 copy-start.51
  493.1 4.3 copy-start.53
  496.0 4.2 copy-start.60
  520.1 158.4 %reduce-scatter.22.cloned.1.call-start = ((), (), s32[]{:S(2)}) async-start(), calls=%async_computation.19 | async-start | bytes 1769472
  521.7 6.2 copy-start.38
  521.7 8.6 copy-start.40
  521.7 16.8 %slice-start = ((s8[6291456]{0:T(1024)(128)(4,1)}), s8[4194304]{0:T(1024)(128)(4,1)S(1)}, s32[]{:S(2)}) async-start(s8[6291456]{0:T(1024)(128)(4,1)} %bitcast.84), calls=%async_computation.22 | async-start | bytes 8388608
  523.8 9.4 copy-start.42
  527.9 7.7 copy-start.44
  530.3 8.2 slice-start.1
  530.3 8.2 copy-start.46
  533.2 6.1 copy-start.48
  535.6 5.1 copy-start.50
  541.5 4.3 copy-start.58
  543.6 4.1 copy-start.72
  547.7 155.0 %reduce-scatter.16.cloned.1.call-start = ((), (), s32[]{:S(2)}) async-start(), calls=%async_computation.16 | async-start | bytes 1769472 | tf_op jit(solution)/shard_map/reduce_scatter | solution.py:226
  549.3 216.1 %reduce-scatter.18.cloned.1.call-start = ((), (), s32[]{:S(2)}) async-start(), calls=%async_computation.17 | async-start | bytes 7077888 | tf_op jit(solution)/shard_map/reduce_scatter | solution.py:238
  554.6 273.9 %reduce-scatter.20.cloned.1.call-start = ((), (), s32[]{:S(2)}) async-start(), calls=%async_computation.18 | async-start | bytes 7077888 | tf_op jit(solution)/shard_map/reduce_scatter | solution.py:244
  560.2 292.7 %reduce-scatter.24.cloned.1.call-start = ((), (), s32[]{:S(2)}) async-start(), calls=%async_computation.20 | async-start | bytes 1769472
  655.7 9.7 copy-start.67
  657.2 9.1 copy-start.62
  657.2 220.3 %reduce-scatter.26.cloned.1.call-start = ((), (), s32[]{:S(2)}) async-start(), calls=%async_computation.21 | async-start | bytes 1769472
  658.7 178.1 %copy-start.64 = (bf16[768,768]{1,0:T(8,128)(2,1)S(1)}, bf16[768,768]{1,0:T(8,128)(2,1)}, u32[]{:S(2)}) copy-start(bf16[768,768]{1,0:T(8,128)(2,1)} %all-gather.20.cloned.1.call-done) | copy-start | bytes 3538948
  838.6 40.2 %copy-start.80 = (bf16[384,768]{1,0:T(8,128)(2,1)S(1)}, bf16[384,768]{1,0:T(8,128)(2,1)}, u32[]{:S(2)}) copy-start(bf16[384,768]{1,0:T(8,128)(2,1)} %reduce-scatter.16.cloned.1.call-done) | copy-start | bytes 1769476
  (51 other events, 148.9 us)
Sparse Core Ops, SparseCore 0:
  9.6 24.8 all-gather.19
  36.0 22.7 all-gather.23
  60.4 22.9 all-gather.17
  86.0 62.2 all-gather.21
  151.0 60.4 all-gather.25
  212.9 20.9 all-gather.27
  235.5 62.6 all-gather.29
  299.7 62.5 all-gather.31
  520.3 133.8 reduce-scatter.13
  656.8 21.6 reduce-scatter.21
  680.9 21.7 reduce-scatter.15
  705.4 59.9 reduce-scatter.17
  768.4 59.9 reduce-scatter.19
  831.1 21.8 reduce-scatter.23
  855.8 21.6 reduce-scatter.25
where the time goes:
time: 1200 us
  waiting for transfers between devices  513 us (43%)
  blocking collectives  340 us (28%)
  matrix products  214 us (18%)
  other arithmetic  72.8 us (6%)
  local copies, waits for them, and re-layouts  38.5 us (3%)
  between operations  16.7 us (1%)
    psum x1, blocking collectives, on_device(): totals = lax.psum(tuple(shards), 'ctx')  304 us
    dot_general x30, matrix products, inner_rows(): lax.dot_general(left, right, (((1,), (1,)), ((), ())), preferred_element_...  94 us
    reduce_scatter x1, waiting for transfers between devices, on_device(): lax.psum_scatter(key_terms.astype(jnp.bfloat16), 'ctx', scatter_dimension...  93.9 us
    reduce_scatter x1, waiting for transfers between devices, on_device(): lax.psum_scatter(grad_outer.astype(jnp.bfloat16), 'fsdp', scatter_dimensi...  63 us
    reduce_scatter x1, waiting for transfers between devices, on_device(): lax.psum_scatter(grad_inner.astype(jnp.bfloat16), 'fsdp', scatter_dimensi...  62.7 us
    convert_element_type x12, other arithmetic, on_device(): d_scores = (probs * (d_probs - delta[:, None])).astype(jnp.bfloat16)  56.2 us
    all_gather x1, waiting for transfers between devices, on_device(): lax.all_gather(key_low, 'ctx', axis=0, tiled=True)  54.9 us
    all_gather x1, waiting for transfers between devices, on_device(): lax.all_gather(inner_weight, 'fsdp', axis=0, tiled=True)  54.8 us
  transfers between devices with their start and end apart: 15, of which 13 were waited for; matrix products, arithmetic and copies ran while one was open for 12% of the time, Pallas kernels for 0%

commit v1 on v0

--- a/solution.py
+++ b/solution.py
@@ -1,12 +1,33 @@
+import functools
 import math
 import jax
 import jax.numpy as jnp
 from jax import lax
 from jax.sharding import PartitionSpec as P
+from jax.lax import axis_index, axis_size, ppermute
 
 H = 12
 HD = 64
 eps = 1e-12
+
+
+def remake_goods(array_here, d_out):
+    z1 = axis_size("ctx")
+    local_next, all_rows, last = (z1, axis_index("ctx"), array_here.shape[d_out])
+    heap = [tick * local_next if ix == d_out else tick for ix, tick in enumerate(array_here.shape)]
+    opened = jnp.zeros(heap, array_here.dtype)
+    z2 = lax.dynamic_update_slice_in_dim(opened, array_here, all_rows * last, axis=d_out)
+    for d in range(1, local_next):
+        array_here = ppermute(
+            array_here, "ctx", list(map(lambda ix: (ix, (ix + 1) % local_next), range(local_next)))
+        )
+        z2 = lax.dynamic_update_slice_in_dim(
+            z2, array_here, (all_rows - d) % local_next * last, axis=d_out
+        )
+    return z2
+
+
+play_samples = functools.partial(remake_goods, d_out=0)
 
 
 def layer_norm(r, gain, shift):
@@ -115,7 +136,7 @@
     places_own = first_row + jnp.arange(rows, dtype=jnp.int32)
     segs_own = segment_of(places_own, doc_lengths[0])
     keys_all, values_all = (
-        lax.all_gather(key_low, "ctx", axis=0, tiled=True),
+        play_samples(key_low),
         lax.all_gather(value_low, "ctx", axis=0, tiled=True),
     )
     places_all = jnp.arange(length_total, dtype=jnp.int32)

time: 1200 us -> 1160 us (0.967)
  waiting for transfers between devices: 513 us -> 440 us
  local copies, waits for them, and re-layouts: 38.5 us -> 62.6 us
  starting transfers between devices: 1.07 us -> 13.2 us
    ppermute x0 -> x15, waiting for transfers between devices: none -> 110 us  [remake_goods(): ppermute(array_here, 'ctx', list(map(lambda ix: (ix, (ix + 1) % local_nex...]
    all_gather x1 -> x0, waiting for transfers between devices: 54.9 us -> none  [on_device(): lax.all_gather(key_low, 'ctx', axis=0, tiled=True)]
    all_gather x1, waiting for transfers between devices: 54.8 us -> 0.02 us  [on_device(): lax.all_gather(inner_weight, 'fsdp', axis=0, tiled=True)]
    all_gather x1, waiting for transfers between devices: 52.7 us -> 0.02 us  [on_device(): lax.all_gather(outer_weight, 'fsdp', axis=0, tiled=True)]
    convert_element_type x12, other arithmetic: 56.2 us -> 34.7 us  [on_device(): d_scores = (probs * (d_probs - delta[:, None])).astype(jnp.bfloat16)]
    all_gather x1, waiting for transfers between devices: 16.8 us -> 0.01 us  [on_device(): lax.all_gather(value_low, 'ctx', axis=0, tiled=True)]
    dynamic_update_slice x0 -> x15, local copies, waits for them, and re-layouts: none -> 15.7 us  [remake_goods(): lax.dynamic_update_slice_in_dim(z2, array_here, (all_rows - d) % local_ne...]
    ppermute x0 -> x15, starting transfers between devices: none -> 12.2 us  [remake_goods(): ppermute(array_here, 'ctx', list(map(lambda ix: (ix, (ix + 1) % local_nex...]
  transfers between devices with their start and end apart: 15 -> 29, of which waited for: 13 -> 21; matrix products, arithmetic and copies ran while one was open for 12% -> 17% of each run, Pallas kernels for 0% -> 0%
where the time goes in v1:
time: 1160 us; the launch traced here: 1150 us
  waiting for transfers between devices  440 us (38%)
  blocking collectives  342 us (29%)
  matrix products  211 us (18%)
  other arithmetic  67.3 us (6%)
  local copies, waits for them, and re-layouts  62.6 us (5%)
  between operations  16.7 us (1%)
  starting transfers between devices  13.2 us (1%)
    psum x1, blocking collectives, on_device(): totals = lax.psum(tuple(shards), 'ctx')  304 us
    ppermute x15, waiting for transfers between devices, remake_goods(): ppermute(array_here, 'ctx', list(map(lambda ix: (ix, (ix + 1) % local_nex...  110 us
    reduce_scatter x1, waiting for transfers between devices, on_device(): lax.psum_scatter(key_terms.astype(jnp.bfloat16), 'ctx', scatter_dimension...  92.2 us
    dot_general x30, matrix products, inner_rows(): lax.dot_general(left, right, (((1,), (1,)), ((), ())), preferred_element_...  83.3 us
    reduce_scatter x1, waiting for transfers between devices, on_device(): lax.psum_scatter(grad_inner.astype(jnp.bfloat16), 'fsdp', scatter_dimensi...  62.9 us
    reduce_scatter x1, waiting for transfers between devices, on_device(): lax.psum_scatter(grad_outer.astype(jnp.bfloat16), 'fsdp', scatter_dimensi...  62.9 us
    dot_general x30, matrix products, inner_cols(): lax.dot_general(left, right, (((0,), (0,)), ((), ())), preferred_element_...  55.5 us
    unnamed x17, waiting for transfers between devices  47.9 us
  transfers between devices with their start and end apart: 29, of which 21 were waited for; matrix products, arithmetic and copies ran while one was open for 17% of the time, Pallas kernels for 0%

profile of v1, /device:TPU:1, one launch (start us, length us, event | category | flops | bytes accessed | tf_op | source)
XLA Modules:
  0.0 1152.6 jit_solution(4829131503897284451)
XLA Ops:
  10.1 3.7 all-gather.1
  13.9 20.5 %all-gather.21.cloned.1.call-done = bf16[768,768]{1,0:T(8,128)(2,1)} async-done(((bf16[384,768]{1,0:T(8,128)(2,1)}), bf16[768,768]{1,0:T(8,128)(2,1)}) %all-gather.21.cloned.1.call-update) | async-done | bytes 1179664 | tf_op jit(solution)/shard_map/all_gather | solution.py:94
  38.4 20.4 %all-gather.19.cloned.1.call-done = bf16[768,768]{1,0:T(8,128)(2,1)} async-done(((bf16[384,768]{1,0:T(8,128)(2,1)}), bf16[768,768]{1,0:T(8,128)(2,1)}) %all-gather.19.cloned.1.call-update) | async-done | bytes 1179664 | tf_op jit(solution)/shard_map/all_gather | solution.py:93
  58.8 3.0 broadcast_in_dim.41
  64.8 4.7 collective-permute-done
  72.0 4.7 collective-permute-done.1
  79.2 5.5 collective-permute-done.2
  86.4 8.2 collective-permute-done.3
  94.7 16.0 %collective-permute-done.4 = bf16[256,768]{1,0:T(8,128)(2,1)S(1)} collective-permute-done((bf16[256,768]{1,0:T(8,128)(2,1)S(1)}, bf16[256,768]{1,0:T(8,128)(2,1)S(1)}, u32[]{:S(2)}, u32[]{:S(2)}) %collective-permute-start.4) | collective-permute-done | bytes 393248 | tf_op jit(solution)/shard_map/ppermute | solution.py:21
  110.7 10.9 collective-permute-done.5
  121.6 18.0 %collective-permute-done.6 = bf16[256,768]{1,0:T(8,128)(2,1)S(1)} collective-permute-done((bf16[256,768]{1,0:T(8,128)(2,1)S(1)}, bf16[256,768]{1,0:T(8,128)(2,1)S(1)}, u32[]{:S(2)}, u32[]{:S(2)}) %collective-permute-start.6) | collective-permute-done | bytes 393248 | tf_op jit(solution)/shard_map/ppermute | solution.py:21
  139.7 14.3 %collective-permute-done.7 = bf16[256,768]{1,0:T(8,128)(2,1)S(1)} collective-permute-done((bf16[256,768]{1,0:T(8,128)(2,1)S(1)}, bf16[256,768]{1,0:T(8,128)(2,1)S(1)}, u32[]{:S(2)}, u32[]{:S(2)}) %collective-permute-start.7) | collective-permute-done | bytes 393248 | tf_op jit(solution)/shard_map/ppermute | solution.py:21
  154.1 5.3 all-gather.6
  159.4 3.2 all-gather.2
  162.5 3.2 all-gather
  167.9 3.5 all-gather.4
  171.5 3.5 all-gather.3
  175.0 3.5 all-gather.7
  178.5 3.2 all-gather.8
  187.2 3.2 all-gather.5
  205.7 11.0 collective-permute-done.11
  219.8 7.0 collective-permute-done.12
  231.9 4.8 collective-permute-done.13
  242.0 4.8 collective-permute-done.14
  247.6 4.0 fusion.292
  251.6 4.4 fusion.293
  258.2 3.2 fusion.295
  261.4 2.9 fusion.296
  264.4 3.2 fusion.297
  267.5 2.9 fusion.298
  270.4 3.2 fusion.299
  273.6 2.9 fusion.300
  276.5 3.2 fusion.301
  279.7 2.9 fusion.302
  282.6 3.2 fusion.303
  285.7 4.8 fusion.36
  290.6 2.9 fusion.37
  301.9 3.6 fusion.146
  333.3 11.7 %multiply_convert_fusion.12 = (bf16[256,3072]{1,0:T(8,128)(2,1)S(1)}, f32[256,3072]{1,0:T(8,128)}, f32[256,3072]{1,0:T(8,128)}) fusion(f32[3072]{0:T(1024)S(1)} %bitcast.86, bf16[768,3072]{1,0:T(8,128)(2,1)} %all-gather.27.cloned.1.call-done, f32[256,768]{1,0:T(8,128)S(1)} %get-tuple-element.154, f32[768]{0:T(1024)S(1)} %reshape.268, ...), kind=kOutput, calls=%fused_computation.174 | convolution fusion | flops 1260847104 | bytes 13389824 | tf_op jit(solution)/shard_map/dot_general | solution.py:170
  345.1 4.4 fusion.305
  352.1 2.7 fusion.287
  400.6 2.8 multiply_convert_fusion.4
  413.4 4.1 multiply_reduce_fusion.1
  417.5 4.9 multiply_convert_fusion.1
  422.5 4.4 multiply_reduce_fusion
  426.8 4.7 multiply_convert_fusion
  431.6 3.1 fusion.3
  434.7 3.1 fusion.5
  474.3 3.3 fusion.113
  484.7 2.9 fusion.121
  490.0 2.9 fusion.125
  495.3 2.8 fusion.129
  507.4 5.6 convolution_convert_fusion.1
  514.5 3.6 convolution_convert_fusion
  518.2 92.2 %reduce-scatter.14.cloned.1.call-done = bf16[256,1536]{0,1:T(8,128)(2,1)} async-done(((bf16[4096,1536]{0,1:T(8,128)(2,1)}), bf16[256,1536]{0,1:T(8,128)(2,1)}) %reduce-scatter.14.cloned.1.call-update) | async-done | bytes 786448 | tf_op jit(solution)/shard_map/reduce_scatter | solution.py:214
  625.1 9.8 reduce-scatter.22.cloned.1.call-done
  636.3 22.6 %reduce-scatter.16.cloned.1.call-done = bf16[384,768]{1,0:T(8,128)(2,1)} async-done(((bf16[768,768]{1,0:T(8,128)(2,1)}), bf16[384,768]{1,0:T(8,128)(2,1)}) %reduce-scatter.16.cloned.1.call-update) | async-done | bytes 589840 | tf_op jit(solution)/shard_map/reduce_scatter | solution.py:247
  658.9 62.9 %reduce-scatter.18.cloned.1.call-done = bf16[384,3072]{1,0:T(8,128)(2,1)} async-done(((bf16[768,3072]{1,0:T(8,128)(2,1)}), bf16[384,3072]{1,0:T(8,128)(2,1)}) %reduce-scatter.18.cloned.1.call-update) | async-done | bytes 2359312 | tf_op jit(solution)/shard_map/reduce_scatter | solution.py:259
  721.8 62.9 %reduce-scatter.20.cloned.1.call-done = bf16[1536,768]{1,0:T(8,128)(2,1)} async-done(((bf16[3072,768]{1,0:T(8,128)(2,1)}), bf16[1536,768]{1,0:T(8,128)(2,1)}) %reduce-scatter.20.cloned.1.call-update) | async-done | bytes 2359312 | tf_op jit(solution)/shard_map/reduce_scatter | solution.py:265
  784.9 6.1 all-reduce.10
  794.9 2.7 fusion.105
  797.6 11.6 %reduce-scatter.24.cloned.1.call-done = bf16[384,768]{1,0:T(8,128)(2,1)} async-done(((bf16[768,768]{1,0:T(8,128)(2,1)}), bf16[384,768]{1,0:T(8,128)(2,1)}) %reduce-scatter.24.cloned.1.call-update) | async-done | bytes 589840
  810.6 23.3 %reduce-scatter.26.cloned.1.call-done = bf16[384,768]{1,0:T(8,128)(2,1)} async-done(((bf16[768,768]{1,0:T(8,128)(2,1)}), bf16[384,768]{1,0:T(8,128)(2,1)}) %reduce-scatter.26.cloned.1.call-update) | async-done | bytes 589840
  835.2 303.9 %all-reduce.12 = (f32[384,768]{0,1:T(8,128)}, f32[384]{0:T(512)}, f32[384,768]{0,1:T(8,128)}, f32[384,768]{0,1:T(8,128)S(1)}, f32[384]{0:T(512)}, /*index=5*/f32...) all-reduce(bf16[384,768]{0,1:T(8,128)(2,1)S(1)} %copy.52, ...), channel_id=1, replica_groups=mesh['ctx'=16,'fsdp'=2] {'ctx'}, use_global_device_ids=true, to_apply=%region_49.50 | all-reduce | flops 3543552 | bytes 21270528 | tf_op jit(solution)/shard_map/psum | solution.py:278
  (438 shorter events, 237.2 us)
Async XLA Ops:
  7.2 27.3 %all-gather.21.cloned.1.call-start = ((), (), s32[]{:S(2)}) async-start(), calls=%async_computation.9 | async-start | bytes 1769472 | tf_op jit(solution)/shard_map/all_gather | solution.py:94
  7.9 50.9 %all-gather.19.cloned.1.call-start = ((), (), s32[]{:S(2)}) async-start(), calls=%async_computation.8 | async-start | bytes 1769472 | tf_op jit(solution)/shard_map/all_gather | solution.py:93
  8.7 193.6 %all-gather.17.cloned.1.call-start = ((), (), s32[]{:S(2)}) async-start(), calls=%async_computation.7 | async-start | bytes 1769472 | tf_op jit(solution)/shard_map/all_gather | solution.py:91
  9.4 292.5 %all-gather.23.cloned.1.call-start = ((), (), s32[]{:S(2)}) async-start(), calls=%async_computation.10 | async-start | bytes 6684672 | tf_op jit(solution)/shard_map/all_gather | solution.py:140
  37.1 293.9 %all-gather.25.cloned.1.call-start = ((), (), s32[]{:S(2)}) async-start(), calls=%async_computation.11 | async-start | bytes 1769472 | tf_op jit(solution)/shard_map/all_gather | solution.py:96
  37.7 24.1 %copy-start.60 = (bf16[1,256,768]{2,1,0:T(8,128)(2,1)S(1)}, bf16[1,256,768]{2,1,0:T(8,128)(2,1)}, u32[]{:S(2)}) copy-start(bf16[1,256,768]{2,1,0:T(8,128)(2,1)} %param.18) | copy-start | bytes 1179652
  37.7 295.5 %all-gather.27.cloned.1.call-start = ((), (), s32[]{:S(2)}) async-start(), calls=%async_computation.12 | async-start | bytes 7077888 | tf_op jit(solution)/shard_map/all_gather | solution.py:100
  38.3 306.7 %all-gather.29.cloned.1.call-start = ((), (), s32[]{:S(2)}) async-start(), calls=%async_computation.13 | async-start | bytes 7077888 | tf_op jit(solution)/shard_map/all_gather | solution.py:102
  38.3 115.7 %copy-start.94 = (bf16[384]{0:T(512)(128)(2,1)S(1)}, bf16[384]{0:T(512)(128)(2,1)}, u32[]{:S(2)}) copy-start(bf16[384]{0:T(512)(128)(2,1)} %param.31) | copy-start | bytes 2308
  38.4 115.7 %copy-start.95 = (bf16[384]{0:T(512)(128)(2,1)S(1)}, bf16[384]{0:T(512)(128)(2,1)}, u32[]{:S(2)}) copy-start(bf16[384]{0:T(512)(128)(2,1)} %param.25) | copy-start | bytes 2308
  38.4 115.7 %copy-start.96 = (bf16[384]{0:T(512)(128)(2,1)S(1)}, bf16[384]{0:T(512)(128)(2,1)}, u32[]{:S(2)}) copy-start(bf16[384]{0:T(512)(128)(2,1)} %param.20) | copy-start | bytes 2308
  38.4 127.5 %copy-start.97 = (bf16[384]{0:T(512)(128)(2,1)S(1)}, bf16[384]{0:T(512)(128)(2,1)}, u32[]{:S(2)}) copy-start(bf16[384]{0:T(512)(128)(2,1)} %param.27) | copy-start | bytes 2308
  63.1 6.5 collective-permute-start
  69.5 7.2 collective-permute-start.1
  76.7 8.0 collective-permute-start.2
  84.8 9.9 collective-permute-start.3
  94.7 16.0 %collective-permute-start.4 = (bf16[256,768]{1,0:T(8,128)(2,1)S(1)}, bf16[256,768]{1,0:T(8,128)(2,1)S(1)}, u32[]{:S(2)}, u32[]{:S(2)}) collective-permute-start(bf16[256,768]{1,0:T(8,128)(2,1)S(1)} %collective-permute-done.3), channel_id=1, source_target_pairs={{0,2},{2,4},{4,6},{6,8},{8,10},{10,12},{12,14},{14,16},{16,18},{18... | collective-permute-start | bytes 1179656 | tf_op jit(solution)/shard_map/ppermute | solution.py:21
  110.7 10.9 collective-permute-start.5
  121.6 18.1 %collective-permute-start.6 = (bf16[256,768]{1,0:T(8,128)(2,1)S(1)}, bf16[256,768]{1,0:T(8,128)(2,1)S(1)}, u32[]{:S(2)}, u32[]{:S(2)}) collective-permute-start(bf16[256,768]{1,0:T(8,128)(2,1)S(1)} %collective-permute-done.5), channel_id=1, source_target_pairs={{0,2},{2,4},{4,6},{6,8},{8,10},{10,12},{12,14},{14,16},{16,18},{18... | collective-permute-start | bytes 1179656 | tf_op jit(solution)/shard_map/ppermute | solution.py:21
  139.7 14.3 %collective-permute-start.7 = (bf16[256,768]{1,0:T(8,128)(2,1)S(1)}, bf16[256,768]{1,0:T(8,128)(2,1)S(1)}, u32[]{:S(2)}, u32[]{:S(2)}) collective-permute-start(bf16[256,768]{1,0:T(8,128)(2,1)S(1)} %collective-permute-done.6), channel_id=1, source_target_pairs={{0,2},{2,4},{4,6},{6,8},{8,10},{10,12},{12,14},{14,16},{16,18},{18... | collective-permute-start | bytes 1179656 | tf_op jit(solution)/shard_map/ppermute | solution.py:21
  154.0 11.8 %collective-permute-start.8 = (bf16[256,768]{1,0:T(8,128)(2,1)S(1)}, bf16[256,768]{1,0:T(8,128)(2,1)}, u32[]{:S(2)}, u32[]{:S(2)}) collective-permute-start(bf16[256,768]{1,0:T(8,128)(2,1)S(1)} %collective-permute-done.7), channel_id=1, source_target_pairs={{0,2},{2,4},{4,6},{6,8},{8,10},{10,12},{12,14},{14,16},{16,18},{18... | collective-permute-start | bytes 1179656 | tf_op jit(solution)/shard_map/ppermute | solution.py:21
  154.0 456.4 %reduce-scatter.14.cloned.1.call-start = ((), (), s32[]{:S(2)}) async-start(), calls=%async_computation.14 | async-start | bytes 13369344 | tf_op jit(solution)/shard_map/reduce_scatter | solution.py:214
  165.8 17.1 %collective-permute-start.9 = (bf16[256,768]{1,0:T(8,128)(2,1)}, bf16[256,768]{1,0:T(8,128)(2,1)}, u32[]{:S(2)}, u32[]{:S(2)}) collective-permute-start(bf16[256,768]{1,0:T(8,128)(2,1)} %collective-permute-done.8), channel_id=1, source_target_pairs={{0,2},{2,4},{4,6},{6,8},{8,10},{10,12},{12,14},{14,16},{16,18},{18... | collective-permute-start | bytes 1179656 | tf_op jit(solution)/shard_map/ppermute | solution.py:21
  182.8 18.3 %collective-permute-start.10 = (bf16[256,768]{1,0:T(8,128)(2,1)}, bf16[256,768]{1,0:T(8,128)(2,1)}, u32[]{:S(2)}, u32[]{:S(2)}) collective-permute-start(bf16[256,768]{1,0:T(8,128)(2,1)} %collective-permute-done.9), channel_id=1, source_target_pairs={{0,2},{2,4},{4,6},{6,8},{8,10},{10,12},{12,14},{14,16},{16,18},{18... | collective-permute-start | bytes 1179656 | tf_op jit(solution)/shard_map/ppermute | solution.py:21
  201.2 15.6 %collective-permute-start.11 = (bf16[256,768]{1,0:T(8,128)(2,1)}, bf16[256,768]{1,0:T(8,128)(2,1)}, u32[]{:S(2)}, u32[]{:S(2)}) collective-permute-start(bf16[256,768]{1,0:T(8,128)(2,1)} %collective-permute-done.10), channel_id=1, source_target_pairs={{0,2},{2,4},{4,6},{6,8},{8,10},{10,12},{12,14},{14,16},{16,18},{18... | collective-permute-start | bytes 1179656 | tf_op jit(solution)/shard_map/ppermute | solution.py:21
  204.1 78.5 %copy-start.83 = (bf16[256,768]{1,0:T(8,128)(2,1)}, bf16[256,768]{1,0:T(8,128)(2,1)S(1)}, u32[]{:S(2)}) copy-start(bf16[256,768]{1,0:T(8,128)(2,1)S(1)} %fusion.108) | copy-start | bytes 1179652
  216.8 10.1 collective-permute-start.12
  218.3 29.3 %copy-start.87 = (s32[4096]{0:T(1024)S(1)}, s32[4096]{0:T(1024)}, u32[]{:S(2)}) copy-start(s32[4096]{0:T(1024)} %convert_reduce_fusion) | copy-start | bytes 49156
  218.3 29.3 %copy-start.98 = (s32[256]{0:T(256)S(1)}, s32[256]{0:T(256)}, u32[]{:S(2)}) copy-start(s32[256]{0:T(256)} %convert_reduce_fusion.1) | copy-start | bytes 3076
  226.8 9.9 collective-permute-start.13
  236.7 10.1 collective-permute-start.14
  258.2 35.3 %copy-start.29 = (f32[256,4096]{1,0:T(8,128)}, f32[256,4096]{1,0:T(8,128)S(1)}, u32[]{:S(2)}) copy-start(f32[256,4096]{1,0:T(8,128)S(1)} %get-tuple-element.134) | copy-start | bytes 12582916
  261.4 32.8 %copy-start.25 = (f32[256,4096]{1,0:T(8,128)}, f32[256,4096]{1,0:T(8,128)S(1)}, u32[]{:S(2)}) copy-start(f32[256,4096]{1,0:T(8,128)S(1)} %get-tuple-element.136) | copy-start | bytes 12582916
  264.3 30.6 %copy-start.21 = (f32[256,4096]{1,0:T(8,128)}, f32[256,4096]{1,0:T(8,128)S(1)}, u32[]{:S(2)}) copy-start(f32[256,4096]{1,0:T(8,128)S(1)} %get-tuple-element.138) | copy-start | bytes 12582916
  267.5 28.1 %copy-start.18 = (f32[256,4096]{1,0:T(8,128)}, f32[256,4096]{1,0:T(8,128)S(1)}, u32[]{:S(2)}) copy-start(f32[256,4096]{1,0:T(8,128)S(1)} %get-tuple-element.140) | copy-start | bytes 12582916
  270.4 26.0 %copy-start.15 = (f32[256,4096]{1,0:T(8,128)}, f32[256,4096]{1,0:T(8,128)S(1)}, u32[]{:S(2)}) copy-start(f32[256,4096]{1,0:T(8,128)S(1)} %get-tuple-element.142) | copy-start | bytes 12582916
  273.6 23.5 %copy-start.12 = (f32[256,4096]{1,0:T(8,128)}, f32[256,4096]{1,0:T(8,128)S(1)}, u32[]{:S(2)}) copy-start(f32[256,4096]{1,0:T(8,128)S(1)} %get-tuple-element.144) | copy-start | bytes 12582916
  276.5 21.4 %copy-start.9 = (f32[256,4096]{1,0:T(8,128)}, f32[256,4096]{1,0:T(8,128)S(1)}, u32[]{:S(2)}) copy-start(f32[256,4096]{1,0:T(8,128)S(1)} %get-tuple-element.146) | copy-start | bytes 12582916
  279.6 18.9 %copy-start.6 = (f32[256,4096]{1,0:T(8,128)}, f32[256,4096]{1,0:T(8,128)S(1)}, u32[]{:S(2)}) copy-start(f32[256,4096]{1,0:T(8,128)S(1)} %get-tuple-element.148) | copy-start | bytes 12582916
  282.6 16.8 %copy-start.3 = (f32[256,4096]{1,0:T(8,128)}, f32[256,4096]{1,0:T(8,128)S(1)}, u32[]{:S(2)}) copy-start(f32[256,4096]{1,0:T(8,128)S(1)} %get-tuple-element.150) | copy-start | bytes 12582916
  285.7 14.9 %copy-start = (f32[256,4096]{1,0:T(8,128)}, f32[256,4096]{1,0:T(8,128)S(1)}, u32[]{:S(2)}) copy-start(f32[256,4096]{1,0:T(8,128)S(1)} %get-tuple-element.152) | copy-start | bytes 12582916
  333.3 11.8 %copy-start.93 = (f32[768]{0:T(1024)S(1)}, f32[768]{0:T(1024)}, u32[]{:S(2)}) copy-start(f32[768]{0:T(1024)} %reshape.270) | copy-start | bytes 9220
  431.6 7.7 copy-start.44
  470.6 164.4 %reduce-scatter.22.cloned.1.call-start = ((), (), s32[]{:S(2)}) async-start(), calls=%async_computation.18 | async-start | bytes 1769472
  472.1 7.7 copy-start.43
  474.3 8.3 copy-start.45
  479.8 7.9 copy-start.49
  482.6 7.5 copy-start.51
  484.7 8.2 copy-start.53
  487.7 7.6 copy-start.55
  490.0 8.1 copy-start.57
  493.0 7.3 copy-start.59
  495.3 8.5 copy-start.62
  505.8 153.1 %reduce-scatter.16.cloned.1.call-start = ((), (), s32[]{:S(2)}) async-start(), calls=%async_computation.15 | async-start | bytes 1769472 | tf_op jit(solution)/shard_map/reduce_scatter | solution.py:247
  507.4 214.4 %reduce-scatter.18.cloned.1.call-start = ((), (), s32[]{:S(2)}) async-start(), calls=%async_computation.16 | async-start | bytes 7077888 | tf_op jit(solution)/shard_map/reduce_scatter | solution.py:259
  513.1 271.6 %reduce-scatter.20.cloned.1.call-start = ((), (), s32[]{:S(2)}) async-start(), calls=%async_computation.17 | async-start | bytes 7077888 | tf_op jit(solution)/shard_map/reduce_scatter | solution.py:265
  518.2 291.1 %reduce-scatter.24.cloned.1.call-start = ((), (), s32[]{:S(2)}) async-start(), calls=%async_computation.19 | async-start | bytes 1769472
  611.9 9.7 copy-start.72
  613.4 9.1 copy-start.66
  613.4 220.4 %reduce-scatter.26.cloned.1.call-start = ((), (), s32[]{:S(2)}) async-start(), calls=%async_computation.20 | async-start | bytes 1769472
  615.0 169.9 %copy-start.91 = (bf16[768]{0:T(1024)(128)(2,1)S(1)}, bf16[768]{0:T(1024)(128)(2,1)}, u32[]{:S(2)}) copy-start(bf16[768]{0:T(1024)(128)(2,1)} %get-tuple-element.87) | copy-start | bytes 4612
  615.0 169.9 %copy-start.92 = (bf16[768]{0:T(1024)(128)(2,1)S(1)}, bf16[768]{0:T(1024)(128)(2,1)}, u32[]{:S(2)}) copy-start(bf16[768]{0:T(1024)(128)(2,1)} %get-tuple-element.118) | copy-start | bytes 4612
  615.0 178.1 %copy-start.69 = (bf16[768,768]{1,0:T(8,128)(2,1)S(1)}, bf16[768,768]{1,0:T(8,128)(2,1)}, u32[]{:S(2)}) copy-start(bf16[768,768]{1,0:T(8,128)(2,1)} %all-gather.19.cloned.1.call-done) | copy-start | bytes 3538948
  794.9 40.3 %copy-start.85 = (bf16[384,768]{1,0:T(8,128)(2,1)S(1)}, bf16[384,768]{1,0:T(8,128)(2,1)}, u32[]{:S(2)}) copy-start(bf16[384,768]{1,0:T(8,128)(2,1)} %reduce-scatter.16.cloned.1.call-done) | copy-start | bytes 1769476
  (70 other events, 244.5 us)
Sparse Core Ops, SparseCore 0:
  9.6 24.8 all-gather.20
  36.0 22.7 all-gather.18
  60.4 22.7 all-gather.16
  85.9 69.9 all-gather.22
  157.3 23.7 all-gather.24
  182.5 62.7 all-gather.26
  246.8 62.7 all-gather.28
  470.7 139.6 reduce-scatter.13
  613.2 21.6 reduce-scatter.21
  637.1 21.7 reduce-scatter.15
  661.8 59.9 reduce-scatter.17
  724.6 59.9 reduce-scatter.19
  787.5 21.6 reduce-scatter.23
  812.0 21.8 reduce-scatter.25
